TPU v7x, 32 devices: a whole 2x2x4 slice. The times are simulated.
32 devices in a mesh: dp: 16 (over z, y, core), tensor: 2 (over x).
Axes of the slice: x: 2, y: 2, z: 4, core: 2. Of those that a mesh axis runs over, the one named last changes fastest.
Arguments:
- tokens: bfloat16 [25088, 512], P(('dp', 'tensor')), may hold values from -6 to 6
- cotangent: bfloat16 [25088, 512], P(('dp', 'tensor')), may hold values from -6 to 6
- ln1_scale: float32 [512], P(('dp', 'tensor')), may hold values from 0.5 to 1.5
- ln1_shift: float32 [512], P(('dp', 'tensor')), may hold values from -1.75 to 1.75
- w_qkv: float32 [3, 512, 512], P(None, ('dp', 'tensor')), may hold values from -0.375 to 0.375
- w_out: float32 [512, 512], P(('dp', 'tensor')), may hold values from -0.75 to 0.75
- out_bias: float32 [512], P(('dp', 'tensor')), may hold values from -0.625 to 0.625
- ln2_scale: float32 [512], P(('dp', 'tensor')), may hold values from 0.5 to 1.5
- ln2_shift: float32 [512], P(('dp', 'tensor')), may hold values from -1.75 to 1.75
- w_router: float32 [512, 32], P(('dp', 'tensor')), may hold values from -0.1875 to 0.1875
- w_in: float32 [32, 512, 2048], P(None, 'dp', 'tensor'), may hold values from -0.25 to 0.25
- b_in: float32 [32, 2048], P('dp', 'tensor'), may hold values from -0.625 to 0.625
- w_back: float32 [32, 2048, 512], P(None, 'tensor', 'dp'), may hold values from -1.5 to 1.5
- b_back: float32 [32, 512], P(None, ('dp', 'tensor')), may hold values from -1.25 to 1.25
- choices: int32 [25088, 2], P(('dp', 'tensor')), may hold values from 0 to 31, as said below
- slots: int32 [25088, 2], P(('dp', 'tensor')), may hold values from -1 to 64, as said below
Outputs:
- result: bfloat16 [25088, 512], P(('dp', 'tensor'))
- grad_tokens: float32 [25088, 512], P(('dp', 'tensor'))
- grad_ln1_scale: float32 [512], P(('dp', 'tensor'))
- grad_ln1_shift: float32 [512], P(('dp', 'tensor'))
- grad_w_qkv: float32 [3, 512, 512], P(None, ('dp', 'tensor'))
- grad_w_out: float32 [512, 512], P(('dp', 'tensor'))
- grad_out_bias: float32 [512], P(('dp', 'tensor'))
- grad_ln2_scale: float32 [512], P(('dp', 'tensor'))
- grad_ln2_shift: float32 [512], P(('dp', 'tensor'))
- grad_w_router: float32 [512, 32], P(('dp', 'tensor'))
- grad_w_in: float32 [32, 512, 2048], P(None, 'dp', 'tensor')
- grad_b_in: float32 [32, 2048], P('dp', 'tensor')
- grad_w_back: float32 [32, 2048, 512], P(None, 'tensor', 'dp')
- grad_b_back: float32 [32, 512], P(None, ('dp', 'tensor'))
Inputs may be any that keep to these rules, and one draw needn't show every extreme that they name: `choices`: each token names two different experts. slots[t, k] is the number of pairs of the same device and expert that come before pair (t, k), where all first choices of the device's 784 tokens in token order come before all its second choices; it is -1 where that number is 65 or more.
All inputs are finite; a program needn't handle non-finite values.
Results may differ from a plain program's by a relative error of at most 0.015.
The roundings to bfloat16 on the way count: a program that leaves them out, or rounds other values in their place, can miss the bound.
Values may be sent and summed in bfloat16 or wider, within the bound.
A program may use at most 320 MiB of HBM per device.

v0:
```python
import functools

import jax
import jax.numpy as jnp
from jax import lax
from jax.experimental import pallas as pl
from jax.experimental.pallas import tpu as pltpu
from jax.sharding import PartitionSpec as P

H = 8
HD = 64
SEQ = 196
CAP = 65
LOW = jnp.bfloat16
WIDE = jnp.float32


def norm_affine(values_in, gain_vec, shift_vec):
    center = values_in - jnp.mean(values_in, axis=-1, keepdims=True)
    spread = jnp.mean(center * center, axis=-1, keepdims=True)
    return center * lax.rsqrt(spread + 1e-06) * gain_vec + shift_vec


MAIN = CAP - 1
GROUP = 4 * MAIN + 16
WIN = 208
STEP = 192


def dot(a, b, dims=((1,), (0,))):
    return lax.dot_general(a, b, (dims, ((), ())), preferred_element_type=WIDE)


NT = ((1,), (1,))
TN = ((0,), (0,))
MESH = pl.DeviceIdType.MESH


def to_tiles(pieces):
    m = pieces[0].shape[0]
    gap = iota((8 * m, m), 0) - 8 * iota((8 * m, m), 1)
    return sum(
        dot(jnp.where(gap == c, 1.0, 0.0).astype(LOW), piece) for c, piece in enumerate(pieces)
    )


def from_tiles(tiles, c, rows):
    gap = iota((rows, tiles.shape[0]), 1) - 8 * iota((rows, tiles.shape[0]), 0)
    return dot(jnp.where(gap == c, 1.0, 0.0).astype(LOW), tiles)


def lane_blocks(v):
    return [v[:, c * 128 : (c + 1) * 128] for c in range(v.shape[1] // 128)]


def split_two(v):
    high = v.astype(LOW)
    return high, (v - high.astype(WIDE)).astype(LOW)


def iota(shape, dim):
    return lax.broadcasted_iota(jnp.int32, shape, dim)


def normalize(v):
    center = v - jnp.mean(v, axis=-1, keepdims=True)
    rstd = lax.rsqrt(jnp.mean(center * center, axis=-1, keepdims=True) + 1e-06)
    return center * rstd, rstd


def norm_back(grad, xhat, rstd, gain):
    inner = grad * gain
    return rstd * (
        inner
        - jnp.mean(inner, axis=-1, keepdims=True)
        - xhat * jnp.mean(inner * xhat, axis=-1, keepdims=True)
    )


def layer_kernel(
    dp, images, experts, tok_ref, cot_ref, choice_ref, slot_ref, gain_one_ref, shift_one_ref,
    bias_ref, gain_two_ref, shift_two_ref, wqkv_ref, wout_ref, router_ref, bback_ref, bin_ref,
    win_ref, wback_ref,
    out_ref, grad_ref, tail_out, dense_out, qkv_out, att_out, lse_out, mid_out, two_out, route_out,
    col_out, dfirst_out, dsecond_out, db_ref,
    dense_ref, lse_ref, mid_ref, route_ref, col_ref, shard_ref, rows_ref,
    wide_ref, low_first, low_second, first_ref, second_ref, b_ref,
    x_ref, g_ref, xs_ref, sg_ref, hid_ref, pre_ref, backs_ref,
    tails_ref, last_ref, x_tiles, g_tiles, xs_tiles, gs_tiles, home_tiles,
    stage_sem, w_send, w_recv, g_send, g_recv, x_send, x_recv, r_send, r_recv,
    t_send, t_recv, c_send, c_recv, s_send, s_recv, a_sems, own_sem, save_sem,
):
    outs_ref = g_ref
    total, width = g_ref.shape
    rows = tok_ref.shape[0]
    qkv_ref = pre_ref.at[0:rows, 0 : 3 * width]
    att_ref = pre_ref.at[0:rows, 3 * width : 4 * width]
    two_ref = hid_ref.at[0:rows, 0:width]
    n = total // MAIN
    tn = n // dp
    parts, _, half = first_ref.shape
    blk_d = low_first.shape[1]
    dense_blk = shard_ref.shape[0]
    groups = n // 4
    per = GROUP
    t_here, d_here = lax.axis_index("tensor"), lax.axis_index("dp")
    me = t_here * dp + d_here
    my_group, my_place = me // 4, me % 4
    core, y_here, z_here = d_here % 2, (d_here // 2) % 2, d_here // 4
    spots, layers = 2 * tn, dp // 4
    spot = y_here * tn + t_here

    def device(p):
        return (p % dp, p // dp)

    def block(p):
        return pl.ds(pl.multiple_of(p * MAIN, 16), MAIN)

    def landing(p):
        return pl.ds(pl.multiple_of(p // 4 * GROUP + p % 4 * MAIN, 16), MAIN)

    tiles = ((x_tiles, xs_tiles), (g_tiles, gs_tiles), (home_tiles, tail_out))

    def tile(which, p, source):
        src, dst = tiles[which]
        return pltpu.make_async_remote_copy(
            src_ref=src.at[p], dst_ref=dst.at[source],
            send_sem=t_send.at[which, p], recv_sem=t_recv.at[which, source],
            device_id=device(p), device_id_type=MESH,
        )

    def own_tile(which):
        src, dst = tiles[which]
        return pltpu.make_async_copy(src.at[me], dst.at[me], own_sem.at[7 + which])

    def weight_rows(p):
        return pl.ds(pl.multiple_of((p % dp) * blk_d, 16), blk_d)

    def weights(which, p, source):
        src, dst = ((low_first, first_ref), (low_second, second_ref))[which]
        return pltpu.make_async_remote_copy(
            src_ref=src.at[p], dst_ref=dst.at[source // dp, weight_rows(source)],
            send_sem=w_send.at[which, p], recv_sem=w_recv.at[which, source],
            device_id=device(p), device_id_type=MESH,
        )

    def own_weights(which):
        src, dst = ((low_first, first_ref), (low_second, second_ref))[which]
        return pltpu.make_async_copy(
            src.at[me], dst.at[t_here, weight_rows(me)], own_sem.at[3 + which]
        )

    def rows_of(which, p, source):
        src, dst, send, recv = (
            (x_ref, xs_ref, x_send, x_recv), (g_ref, sg_ref, g_send, g_recv)
        )[which]
        return pltpu.make_async_remote_copy(
            src_ref=src.at[block(p)], dst_ref=dst.at[landing(source)],
            send_sem=send.at[p], recv_sem=recv.at[source],
            device_id=device(p), device_id_type=MESH,
        )

    def home(which, p, source):
        src, dst = ((outs_ref, out_ref), (backs_ref, grad_ref))[which]
        return pltpu.make_async_remote_copy(
            src_ref=src.at[block(p)], dst_ref=dst.at[block(source)],
            send_sem=r_send.at[which, p], recv_sem=r_recv.at[which, source],
            device_id=device(p), device_id_type=MESH,
        )

    def own(which):
        src, dst = (
            (x_ref, xs_ref), (outs_ref, out_ref), (backs_ref, grad_ref),
            None, None, (g_ref, sg_ref),
        )[which]
        place = block(me) if which in (1, 2) else landing(me)
        return pltpu.make_async_copy(src.at[block(me)], dst.at[place], own_sem.at[which])

    def to_layer(z, source):
        return pltpu.make_async_remote_copy(
            src_ref=shard_ref, dst_ref=dense_ref.at[source, y_here, core, t_here],
            send_sem=c_send.at[z], recv_sem=c_recv.at[source],
            device_id=((z * 2 + y_here) * 2 + core, t_here), device_id_type=MESH,
        )

    def to_spot(s, source):
        return pltpu.make_async_remote_copy(
            src_ref=dense_ref.at[:, y_here, core, t_here],
            dst_ref=dense_ref.at[:, source // tn, core, source % tn],
            send_sem=s_send.at[s], recv_sem=s_recv.at[source],
            device_id=((z_here * 2 + s // tn) * 2 + core, s % tn), device_id_type=MESH,
        )

    def to_core(source):
        return pltpu.make_async_remote_copy(
            src_ref=dense_ref.at[:, :, core], dst_ref=dense_ref.at[:, :, source],
            send_sem=a_sems.at[0], recv_sem=a_sems.at[1],
            device_id=(d_here + 1 - 2 * core, t_here), device_id_type=MESH,
        )

    own_shard = pltpu.make_async_copy(
        shard_ref, dense_ref.at[z_here, y_here, core, t_here], own_sem.at[6]
    )
    pieces = wide_ref.shape[1]
    chunks = n // pieces

    def stage(which, j):
        src = (win_ref, wback_ref)[which]
        c = (me // pieces + j) % chunks
        return pltpu.make_async_copy(
            src.at[pl.ds(c * pieces, pieces)], wide_ref.at[j % 2], stage_sem.at[j % 2]
        )

    barrier = pltpu.get_barrier_semaphore()

    @pl.loop(1, n)
    def _(r):
        pl.semaphore_signal(barrier, inc=1, device_id=device((me + r) % n), device_id_type=MESH)

    stage(0, 0).start()
    for j in range(3):
        shard_ref[:, j * width : (j + 1) * width] = wqkv_ref[j].astype(LOW)
    shard_ref[:, 3 * width : 4 * width] = wout_ref[...].astype(LOW)
    diagonal = iota((dense_blk, dense_blk), 0) == iota((dense_blk, dense_blk), 1)
    lanes = iota((1, 128), 1)
    spread = iota((experts, 128), 1) - iota((experts, 128), 0)
    misc = dot(router_ref[...].astype(LOW), jnp.where(spread == 0, 1.0, 0.0).astype(LOW))
    misc = misc + dot(
        bback_ref[...].astype(LOW), jnp.where(spread == experts, 1.0, 0.0).astype(LOW)
    )
    vectors = (gain_one_ref, shift_one_ref, bias_ref, gain_two_ref, shift_two_ref)
    for i, vec in enumerate(vectors):
        column = jnp.sum(jnp.where(diagonal, vec[...], 0.0), axis=1, keepdims=True)
        misc = jnp.where(lanes == 64 + i, column, misc)
    shard_ref[:, 4 * width : 4 * width + 128] = misc.astype(LOW)
    lines = half // 128
    slab = jnp.zeros((dense_blk, 128), WIDE)
    for i in range(dense_blk):
        part = bin_ref[i // lines : i // lines + 1, (i % lines) * 128 : (i % lines + 1) * 128]
        slab = jnp.where(iota((dense_blk, 1), 0) == i, part, slab)
    shard_ref[:, 4 * width + 128 : 4 * width + 256] = slab.astype(LOW)
    slot_in = slot_ref[...]
    rows_ref[...] = jnp.where(
        (slot_in >= 0) & (slot_in < MAIN), choice_ref[...] * MAIN + slot_in, -1
    )
    last_ref[...] = jnp.where(slot_in == MAIN, choice_ref[...], -1)
    pick = iota((2, 128), 1) - iota((2, 128), 0)
    turned = dot(
        choice_ref[...].astype(WIDE).astype(LOW), jnp.where(pick == 0, 1.0, 0.0).astype(LOW), TN
    ) + dot(slot_ref[...].astype(WIDE).astype(LOW), jnp.where(pick == 2, 1.0, 0.0).astype(LOW), TN)
    col_ref[...] = turned.astype(jnp.int32)
    own_shard.start()
    db_ref[...] = jnp.zeros_like(db_ref)
    pl.semaphore_wait(barrier, n - 1)
    for i in range(1, layers):
        to_layer((z_here + i) % layers, z_here).start()

    def send_weights(which):
        low = (low_first, low_second)[which]
        for j in range(chunks):
            if j + 1 < chunks:
                stage(which, j + 1).start()
            elif which == 0:
                stage(1, 0).start()
            stage(which, j).wait()
            c = (me // pieces + j) % chunks
            low[pl.ds(c * pieces, pieces)] = wide_ref[j % 2].astype(LOW)

            @pl.loop(0, pieces)
            def _(i):
                p = c * pieces + (me + i) % pieces

                @pl.when(p != me)
                def _():
                    weights(which, p, me).start()

        own_weights(which).start()

    send_weights(0)
    own_shard.wait()
    for i in range(1, layers):
        z = (z_here + i) % layers
        to_layer(z, z).wait_recv()
    for i in range(1, spots):
        to_spot((spot + i) % spots, spot).start()
    send_weights(1)

    some = 8
    big = some * MAIN
    place = iota((n, rows), 0)
    last_hit = (place == last_ref[0:1, :]) | (place == last_ref[1:2, :])
    tails_ref[...] = jnp.where(last_hit, 1.0, 0.0).astype(LOW)
    got = dot(tails_ref[...], cot_ref[...]).astype(LOW)
    g_tiles[...] = to_tiles(lane_blocks(got)).reshape(n, 8, 128).astype(LOW)

    @pl.loop(0, n // some)
    def _(j):
        c = (me // some + j) % (n // some)
        place = iota((big, rows), 0) + c * big
        hit = (place == rows_ref[0:1, :]) | (place == rows_ref[1:2, :])
        got = dot(jnp.where(hit, 1.0, 0.0).astype(LOW), cot_ref[...])
        g_ref[pl.ds(pl.multiple_of(c * big, 16), big), :] = got.astype(LOW)

        @pl.loop(0, some)
        def _(i):
            p = c * some + (me + i) % some

            @pl.when(p != me)
            def _():
                rows_of(1, p, me).start()
                tile(1, p, me).start()

    own(5).start()
    own_tile(1).start()
    for i in range(1, spots):
        s = (spot + i) % spots
        to_spot(s, s).wait_recv()
    to_core(core).start()
    to_core(1 - core).wait_recv()

    def dense(cols):
        return dense_ref[:, :, :, :, :, cols].reshape(width, -1)

    misc = dense(slice(4 * width, 4 * width + 128))
    misc_t = misc.astype(WIDE).T
    gain_one, shift_one, bias, gain_two, shift_two = [
        misc_t[64 + i : 65 + i, :] for i in range(5)
    ]
    base = tok_ref[...].astype(WIDE)
    xhat, _ = normalize(base)
    one = (xhat * gain_one + shift_one).astype(LOW)
    for j in range(3):
        cols = slice(j * width, (j + 1) * width)
        qkv_ref[:, cols] = dot(one, dense(cols)).astype(LOW)
    att_ref[...] = jnp.zeros((rows, width), LOW)
    lse_ref[...] = jnp.zeros_like(lse_ref)
    low_half = iota((1, 128), 1) < HD

    @pl.loop(0, images)
    def _(i):
        win = pl.ds(pl.multiple_of(i * STEP, 16), WIN)
        first = i * (SEQ - STEP)
        key_pos = iota((1, WIN), 1)
        key_ok = (key_pos >= first) & (key_pos < first + SEQ)
        row_pos = iota((WIN, 1), 0)
        row_ok = (row_pos >= first) & (row_pos < first + SEQ)
        lse = jnp.zeros((WIN, 128), WIDE)
        for pair in range(H // 2):
            q = qkv_ref[win, pair * 128 : (pair + 1) * 128]
            k = qkv_ref[win, width + pair * 128 : width + (pair + 1) * 128]
            v = qkv_ref[win, 2 * width + pair * 128 : 2 * width + (pair + 1) * 128]
            outs = []
            for side in range(2):
                mask = low_half if side == 0 else jnp.logical_not(low_half)
                qm = jnp.where(mask, q, jnp.zeros_like(q))
                s = jnp.where(key_ok, dot(qm, k, NT) * HD**-0.5, -1e30)
                top = jnp.max(s, axis=-1, keepdims=True)
                p = jnp.exp(s - top)
                all_p = jnp.sum(p, axis=-1, keepdims=True)
                p = (p / all_p).astype(LOW)
                outs.append(dot(p, v))
                lane = iota((1, 128), 1) == 2 * pair + side
                lse = jnp.where(lane, top + jnp.log(all_p), lse)
            got = jnp.where(low_half, outs[0], outs[1]).astype(LOW)
            cols = slice(pair * 128, (pair + 1) * 128)
            att_ref[win, cols] = jnp.where(row_ok, got, att_ref[win, cols])
        lse_ref[win, :] = jnp.where(row_ok, lse, lse_ref[win, :])

    mid = base + dot(att_ref[...], dense(slice(3 * width, 4 * width))) + bias
    mid_ref[...] = mid
    xhat, _ = normalize(mid)
    two = (xhat * gain_two + shift_two).astype(LOW)
    two_ref[...] = two
    lanes = iota((1, 128), 1)
    logits = jnp.where(lanes < experts, dot(two, misc), -1e30)
    route = jnp.exp(logits - jnp.max(logits, axis=-1, keepdims=True))
    route = route / jnp.sum(route, axis=-1, keepdims=True)
    route_ref[...] = route
    high, low = jnp.zeros((128, 128), WIDE), jnp.zeros((128, 128), WIDE)
    for k in range(2):
        chosen = lanes == col_ref[:, k : k + 1]
        gate = jnp.where(chosen, route, 0.0)
        here = jnp.where(lanes == col_ref[:, 2 + k : 3 + k], 1.0, 0.0).astype(LOW)
        part_high, part_low = split_two(gate)
        high = high + dot(part_high, here, TN)
        low = low + dot(part_low, here, TN)
    last = lane_blocks(dot(tails_ref[...], two_ref[...]).astype(LOW))
    last = last + [high[:experts].astype(LOW), low[:experts].astype(LOW)]
    x_tiles[...] = to_tiles(last).reshape(n, 8, 128).astype(LOW)

    @pl.loop(0, n // some)
    def _(c):
        place = iota((big, rows), 0) + c * big
        hit = (place == rows_ref[0:1, :]) | (place == rows_ref[1:2, :])
        got = dot(jnp.where(hit, 1.0, 0.0).astype(LOW), two_ref[...])
        x_ref[pl.ds(pl.multiple_of(c * big, 16), big), :] = got.astype(LOW)

    def others(j, action):
        for i in range(4):
            if isinstance(j, int) and j == 0:
                if i > 0:
                    action(4 * my_group + (my_place + i) % 4)
            else:
                action(4 * ((my_group + groups + j) % groups) + (my_place + i) % 4)

    def send_slots(p):
        tile(0, p, me).start()
        rows_of(0, p, me).start()

    own(0).start()
    own_tile(0).start()
    others(0, send_slots)

    @pl.loop(1, groups)
    def _(j):
        others(groups - j, send_slots)

    saved = (
        (dense_ref, dense_out), (qkv_ref, qkv_out), (att_ref, att_out), (lse_ref, lse_out),
        (mid_ref, mid_out), (two_ref, two_out), (route_ref, route_out), (col_ref, col_out),
        (low_first, dfirst_out), (low_second, dsecond_out),
    )

    def save(i):
        return pltpu.make_async_copy(saved[i][0], saved[i][1], save_sem.at[i])

    for i in range(8):
        save(i).start()

    per_dp = experts // dp
    for f in range(parts):
        place = me // per_dp
        slab = dense_ref[
            place // 4, (place // 2) % 2, place % 2, f, :, 4 * width + 128 : 4 * width + 256
        ].astype(WIDE)
        lines = dense_blk // per_dp
        mine = slab[:lines]
        for i in range(1, per_dp):
            mine = jnp.where(me % per_dp == i, slab[i * lines : (i + 1) * lines], mine)
        for i in range(lines):
            b_ref[:, f * half + i * 128 : f * half + (i + 1) * 128] = mine[i : i + 1]

    for i in range(8):
        save(i).wait()
    own_weights(0).wait()
    own_weights(1).wait()
    own(5).wait()
    own_tile(1).wait()

    @pl.loop(1, n)
    def _(r):
        p = (me + r) % n
        for which in range(2):
            weights(which, p, p).wait_recv()
            weights(which, p, me).wait_send()
        rows_of(1, p, me).wait_send()

    place = iota((per, 1), 0)
    sender = jnp.where(place < 4 * MAIN, place // MAIN, place - 4 * MAIN)
    slot_at = jnp.where(place < 4 * MAIN, place % MAIN, MAIN)

    def flat(ref, group):
        return ref[pl.ds(4 * group, 4)].astype(WIDE).reshape(32, 128).astype(LOW)

    def compute(group):
        here = pl.ds(pl.multiple_of(group * per, 16), per)
        tail = pl.ds(pl.multiple_of(group * per + 4 * MAIN, 16), 16)
        x_last, g_last = flat(xs_tiles, group), flat(gs_tiles, group)
        for c in range(width // 128):
            cols = slice(c * 128, (c + 1) * 128)
            xs_ref[tail, cols] = from_tiles(x_last, c, 16).astype(LOW)
            sg_ref[tail, cols] = from_tiles(g_last, c, 16).astype(LOW)
        gates = from_tiles(x_last, width // 128, 16) + from_tiles(x_last, width // 128 + 1, 16)
        x = xs_ref[here, :]
        lanes = iota((1, 128), 1)
        gate = jnp.zeros((per, 1), WIDE)
        for s in range(4):
            got = jnp.sum(jnp.where(lanes == slot_at, gates[s : s + 1], 0.0), axis=1, keepdims=True)
            gate = jnp.where(sender == s, got, gate)
        sg = (gate * sg_ref[here, :].astype(WIDE)).astype(LOW)
        sg_ref[here, :] = sg
        out = jnp.zeros((per, width), WIDE)
        back = jnp.zeros((per, width), WIDE)
        for f in range(parts):
            cols = slice(f * half, (f + 1) * half)
            pre = dot(x, first_ref[f]) + b_ref[:, cols]
            t = jnp.tanh(0.7978845608028654 * (pre + 0.044715 * (pre * pre * pre)))
            hid = (0.5 * pre * (1.0 + t)).astype(LOW)
            slope = 0.5 * (1.0 + t) + (0.5 * pre) * (1.0 - t * t) * (
                0.7978845608028654 * (1.0 + 0.134145 * (pre * pre))
            )
            hid_ref[here, cols] = hid
            out = out + dot(hid, second_ref[f], NT)
            gp = (dot(sg, second_ref[f]) * slope).astype(LOW)
            pre_ref[here, cols] = gp
            db_ref[:, cols] += jnp.sum(gp.astype(WIDE), axis=0, keepdims=True)
            back = back + dot(gp, first_ref[f], NT)
        out, back = out.astype(LOW), back.astype(LOW)
        main = pl.ds(pl.multiple_of(group * 4 * MAIN, 16), 4 * MAIN)
        outs_ref[main, :] = out[: 4 * MAIN]
        backs_ref[main, :] = back[: 4 * MAIN]
        made = to_tiles(lane_blocks(out[4 * MAIN :]) + lane_blocks(back[4 * MAIN :]))
        home_tiles[pl.ds(4 * group, 4)] = made[:32].reshape(4, 8, 128).astype(LOW)

    def send_home(j):
        def both(p):
            home(0, p, me).start()
            home(1, p, me).start()
            tile(2, p, me).start()

        others(j, both)

    def arrived(p):
        for which in range(2):
            rows_of(which, p, p).wait_recv()
            tile(which, p, p).wait_recv()

    own(0).wait()
    own_tile(0).wait()
    others(0, arrived)
    compute(my_group)
    own(1).start()
    own(2).start()
    own_tile(2).start()
    send_home(0)

    @pl.loop(1, groups)
    def _(j):
        others(j, arrived)
        compute((my_group + j) % groups)
        send_home(j)

    for f in range(parts):
        mine = slice(f * dp, (f + 1) * dp)
        for q in range(half // 256):
            cols = slice(f * half + q * 256, f * half + (q + 1) * 256)
            sub = slice(q * 256, (q + 1) * 256)
            low_first[mine, :, sub] = (
                dot(xs_ref[...], pre_ref[:, cols], TN).astype(LOW).reshape(dp, blk_d, 256)
            )
            low_second[mine, :, sub] = (
                dot(sg_ref[...], hid_ref[:, cols], TN).astype(LOW).reshape(dp, blk_d, 256)
            )
    save(8).start()
    save(9).start()
    save(8).wait()
    save(9).wait()
    own(1).wait()
    own(2).wait()
    own_tile(2).wait()
    to_core(core).wait_send()
    for i in range(1, spots):
        to_spot((spot + i) % spots, spot).wait_send()
    for i in range(1, layers):
        to_layer((z_here + i) % layers, z_here).wait_send()

    @pl.loop(1, n)
    def _(r):
        p = (me + r) % n
        rows_of(0, p, me).wait_send()
        for which in range(2):
            home(which, p, me).wait_send()
            home(which, p, p).wait_recv()
        for which in range(3):
            tile(which, p, me).wait_send()
        tile(2, p, p).wait_recv()


def backward_kernel(
    dp, images, experts, tok_in, cot_in, dense_in, qkv_in, att_in, lse_in, mid_in,
    two_in, route_in, col_in, out_in, grad_in, tiles_in, db_ref, dfirst_ref, dsecond_ref,
    result_ref, dtok_ref, done_ref, gin_ref, gback_ref,
    tok_ref, cot_ref, dense_ref, qkv_ref, att_ref, lse_ref, mid_ref,
    two_ref, route_ref, col_ref, out_ref, grad_ref, tiles_ref, in_sem,
    dmid_ref, datt_ref, dqkv_ref, ddense_ref, got_a, sum_a, got_b, sum_b, got_c,
    w_send, w_recv, own_sem, a_sems, b_send, b_recv, c_send, c_recv,
):
    rows, width = tok_ref.shape
    n = dfirst_ref.shape[0]
    tn = n // dp
    t_here, d_here = lax.axis_index("tensor"), lax.axis_index("dp")
    me = t_here * dp + d_here
    core, y_here, z_here = d_here % 2, (d_here // 2) % 2, d_here // 4
    spots, layers = 2 * tn, dp // 4
    spot = y_here * tn + t_here

    def device(p):
        return (p % dp, p // dp)

    def grads_to(which, p):
        src, dst = ((dfirst_ref, gin_ref), (dsecond_ref, gback_ref))[which]
        return pltpu.make_async_remote_copy(
            src_ref=src.at[p], dst_ref=dst.at[me],
            send_sem=w_send.at[which, p], recv_sem=w_recv.at[which, me],
            device_id=device(p), device_id_type=MESH,
        )

    def grads_from(which, p):
        src, dst = ((dfirst_ref, gin_ref), (dsecond_ref, gback_ref))[which]
        return pltpu.make_async_remote_copy(
            src_ref=src.at[p], dst_ref=dst.at[p],
            send_sem=w_send.at[which, p], recv_sem=w_recv.at[which, p],
            device_id=device(p), device_id_type=MESH,
        )

    def own(which):
        src, dst = ((dfirst_ref, gin_ref), (dsecond_ref, gback_ref))[which]
        return pltpu.make_async_copy(src.at[me], dst.at[me], own_sem.at[which])

    def to_spot(s):
        return pltpu.make_async_remote_copy(
            src_ref=sum_a.at[:, s], dst_ref=got_b.at[spot],
            send_sem=b_send.at[s], recv_sem=b_recv.at[spot],
            device_id=((z_here * 2 + s // tn) * 2 + core, s % tn), device_id_type=MESH,
        )

    def from_spot(s):
        return pltpu.make_async_remote_copy(
            src_ref=sum_a.at[:, s], dst_ref=got_b.at[s],
            send_sem=b_send.at[s], recv_sem=b_recv.at[s],
            device_id=((z_here * 2 + s // tn) * 2 + core, s % tn), device_id_type=MESH,
        )

    def to_layer(z):
        return pltpu.make_async_remote_copy(
            src_ref=sum_b.at[z], dst_ref=got_c.at[z_here],
            send_sem=c_send.at[z], recv_sem=c_recv.at[z_here],
            device_id=((z * 2 + y_here) * 2 + core, t_here), device_id_type=MESH,
        )

    def from_layer(z):
        return pltpu.make_async_remote_copy(
            src_ref=sum_b.at[z], dst_ref=got_c.at[z],
            send_sem=c_send.at[z], recv_sem=c_recv.at[z],
            device_id=((z * 2 + y_here) * 2 + core, t_here), device_id_type=MESH,
        )

    slots_main = out_in.shape[0]
    moves = (
        (out_in, out_ref.at[0:slots_main]), (grad_in, grad_ref.at[0:slots_main]),
        (tiles_in, tiles_ref), (cot_in, cot_ref), (route_in, route_ref), (mid_in, mid_ref),
        (col_in, col_ref), (two_in, two_ref), (dense_in, dense_ref), (att_in, att_ref),
        (qkv_in, qkv_ref), (lse_in, lse_ref), (tok_in, tok_ref),
    )

    def bring(i):
        return pltpu.make_async_copy(moves[i][0], moves[i][1], in_sem.at[i])

    barrier = pltpu.get_barrier_semaphore()

    @pl.loop(1, n)
    def _(r):
        pl.semaphore_signal(barrier, inc=1, device_id=device((me + r) % n), device_id_type=MESH)

    for i in range(len(moves)):
        bring(i).start()
    pl.semaphore_wait(barrier, n - 1)

    @pl.loop(1, n)
    def _(r):
        grads_to(0, (me + r) % n).start()

    @pl.loop(1, 3 * n // 8)
    def _(r):
        grads_to(1, (me + r) % n).start()

    own(0).start()
    own(1).start()

    def put(cols, val):
        ddense_ref[:, :, :, cols] = val.reshape(ddense_ref.shape[:3] + (-1,)).astype(LOW)

    for i in range(len(moves)):
        bring(i).wait()
    tiles = tiles_ref[...].astype(WIDE).reshape(8 * n, 128).astype(LOW)
    rest = out_ref.shape[0] - slots_main
    for c in range(width // 128):
        cols = slice(c * 128, (c + 1) * 128)
        out_ref[slots_main:, cols] = from_tiles(tiles, c, rest).astype(LOW)
        grad_ref[slots_main:, cols] = from_tiles(tiles, width // 128 + c, rest).astype(LOW)

    misc_t = dense_ref[:, 4 * width : 4 * width + 128].astype(WIDE).T
    misc_low = misc_t.astype(LOW)
    gain_one, shift_one, bias, gain_two, shift_two = [
        misc_t[64 + i : 65 + i, :] for i in range(5)
    ]
    lanes = iota((1, 128), 1)
    per = 112
    slots_all = out_ref.shape[0]

    def chunk(c, carry):
        d_router, d_bias_back, d_gain, d_shift, d_bias = carry
        here = pl.ds(pl.multiple_of(c * per, 16), per)
        g = cot_ref[here, :]
        gw = g.astype(WIDE)
        route = route_ref[here, :]
        mid = mid_ref[here, :]
        result = mid
        probs = jnp.zeros((per, 128), WIDE)
        gate_sel = jnp.zeros((per, 128), WIDE)
        both = jnp.zeros((per, slots_all), WIDE)
        for k in range(2):
            choice = col_ref[here, k : k + 1]
            slot = col_ref[here, 2 + k : 3 + k]
            kept = slot >= 0
            chosen = (lanes == choice) & kept
            where_to = jnp.where(slot < MAIN, choice * MAIN + slot, slots_main + choice)
            where_to = jnp.where(kept, where_to, -1)
            hit = jnp.where(iota((per, slots_all), 1) == where_to, 1.0, 0.0)
            both = both + hit
            add_b = jnp.where((lanes == choice + experts) & kept, 1.0, 0.0).astype(LOW)
            picked = dot(hit.astype(LOW), out_ref[...]) + dot(add_b, misc_low)
            gate = jnp.sum(jnp.where(chosen, route, 0.0), axis=1, keepdims=True)
            result = result + gate * picked
            gg = jnp.sum(gw * picked, axis=1, keepdims=True)
            probs = probs + jnp.where(chosen, gg, 0.0)
            gate_sel = gate_sel + jnp.where(chosen, route, 0.0)
        result_ref[here, :] = result.astype(LOW)
        logits = route * (probs - jnp.sum(probs * route, axis=-1, keepdims=True))
        high, low = split_two(logits)
        d_two = dot(both.astype(LOW), grad_ref[...]) + dot(high, misc_low) + dot(low, misc_low)
        two = two_ref[here, :]
        d_router = d_router + dot(high, two, TN) + dot(low, two, TN)
        gs_high, gs_low = split_two(gate_sel)
        d_bias_back = d_bias_back + dot(gs_high, g, TN) + dot(gs_low, g, TN)
        xhat, rstd = normalize(mid)
        d_gain = d_gain + jnp.sum(d_two * xhat, axis=0, keepdims=True)
        d_shift = d_shift + jnp.sum(d_two, axis=0, keepdims=True)
        d_mid = gw + norm_back(d_two, xhat, rstd, gain_two)
        d_bias = d_bias + jnp.sum(d_mid, axis=0, keepdims=True)
        dtok_ref[here, :] = d_mid
        dmid_ref[here, :] = d_mid.astype(LOW)
        return d_router, d_bias_back, d_gain, d_shift, d_bias

    zero = jnp.zeros((1, width), WIDE)
    wide_zero = jnp.zeros((128, width), WIDE)
    d_router, d_bias_back, d_gain_two, d_shift_two, d_bias = lax.fori_loop(
        0, rows // per, chunk, (wide_zero, wide_zero, zero, zero, zero)
    )
    out_cols = slice(3 * width, 4 * width)
    datt_ref[...] = dot(dmid_ref[...], dense_ref[:, out_cols], NT).astype(LOW)
    put(out_cols, dot(att_ref[...], dmid_ref[...], TN))
    dqkv_ref[...] = jnp.zeros_like(dqkv_ref)
    low_half = iota((1, 128), 1) < HD

    @pl.loop(0, images)
    def _(i):
        win = pl.ds(pl.multiple_of(i * STEP, 16), WIN)
        first = i * (SEQ - STEP)
        key_pos = iota((1, WIN), 1)
        key_ok = (key_pos >= first) & (key_pos < first + SEQ)
        row_pos = iota((WIN, 1), 0)
        row_ok = (row_pos >= first) & (row_pos < first + SEQ)
        lse = lse_ref[win, :]
        for pair in range(H // 2):
            cols = [
                slice(j * width + pair * 128, j * width + (pair + 1) * 128) for j in range(3)
            ]
            q, k, v = [qkv_ref[win, c] for c in cols]
            do = datt_ref[win, pair * 128 : (pair + 1) * 128]
            do = jnp.where(row_ok, do, jnp.zeros_like(do))
            dq, dk, dv = [jnp.zeros((WIN, 128), WIDE) for _ in range(3)]
            for half in range(2):
                mask = low_half if half == 0 else jnp.logical_not(low_half)
                qm, km, dom = [jnp.where(mask, a, jnp.zeros_like(a)) for a in (q, k, do)]
                h = 2 * pair + half
                s = dot(qm, k, NT) * HD**-0.5
                p = jnp.where(key_ok & row_ok, jnp.exp(jnp.minimum(s - lse[:, h : h + 1], 0.0)), 0.0)
                dp = dot(dom, v, NT)
                delta = jnp.sum(dp * p, axis=-1, keepdims=True)
                ds = (p * (dp - delta) * HD**-0.5).astype(LOW)
                dv = dv + dot(p.astype(LOW), dom, TN)
                dq = dq + dot(ds, km)
                dk = dk + dot(ds, qm, TN)
            for c, val in zip(cols, (dq, dk, dv)):
                dqkv_ref[win, c] = jnp.where(row_ok, val.astype(LOW), dqkv_ref[win, c])

    xhat, rstd = normalize(tok_ref[...].astype(WIDE))
    one = (xhat * gain_one + shift_one).astype(LOW)
    d_one = jnp.zeros((rows, width), WIDE)
    for j in range(3):
        cols = slice(j * width, (j + 1) * width)
        put(cols, dot(one, dqkv_ref[:, cols], TN))
        d_one = d_one + dot(dqkv_ref[:, cols], dense_ref[:, cols], NT)
    d_gain_one = jnp.sum(d_one * xhat, axis=0, keepdims=True)
    d_shift_one = jnp.sum(d_one, axis=0, keepdims=True)
    dtok_ref[...] = dtok_ref[...] + norm_back(d_one, xhat, rstd, gain_one)
    row = iota((128, 1), 0)
    grads = jnp.where(row < experts, d_router, 0.0)
    moved = jnp.concatenate([d_bias_back[128 - experts :], d_bias_back[: 128 - experts]], axis=0)
    grads = grads + jnp.where((row >= experts) & (row < 2 * experts), moved, 0.0)
    for i, vec in enumerate((d_gain_one, d_shift_one, d_bias, d_gain_two, d_shift_two)):
        grads = grads + jnp.where(row == 64 + i, vec, 0.0)
    put(slice(4 * width, 4 * width + 128), grads.T)
    per_dp = experts // dp
    lines = ddense_ref.shape[2] // tn // per_dp
    count = tn * lines
    line = iota((count, 1), 0)
    slab = jnp.zeros((count, 128), WIDE)
    for i in range(count):
        slab = jnp.where(line == i, db_ref[:, i * 128 : (i + 1) * 128], slab)
    line = iota((width, count), 1)
    place = (me // per_dp * tn + line // lines) * (lines * per_dp) + me % per_dp * lines + line % lines
    placed = jnp.where(iota((width, count), 0) == place, 1.0, 0.0).astype(LOW)
    put(slice(4 * width + 128, 4 * width + 256), dot(placed, slab.astype(LOW)))

    partner = pltpu.make_async_remote_copy(
        src_ref=ddense_ref.at[:, 1 - core], dst_ref=got_a,
        send_sem=a_sems.at[0], recv_sem=a_sems.at[1],
        device_id=(d_here + 1 - 2 * core, t_here), device_id_type=MESH,
    )
    partner.start()
    partner.wait()
    total = ddense_ref[:, core].astype(WIDE) + got_a[...].astype(WIDE)
    sum_a[...] = total.reshape(sum_a.shape).astype(LOW)
    for i in range(1, spots):
        to_spot((spot + i) % spots).start()

    @pl.loop(3 * n // 8, 3 * n // 4)
    def _(r):
        grads_to(1, (me + r) % n).start()

    total = sum_a[:, spot].astype(WIDE)
    for i in range(1, spots):
        s = (spot + i) % spots
        from_spot(s).wait_recv()
        total = total + got_b[s].astype(WIDE)
    sum_b[...] = total.astype(LOW)
    for i in range(1, layers):
        to_layer((z_here + i) % layers).start()

    @pl.loop(3 * n // 4, n)
    def _(r):
        grads_to(1, (me + r) % n).start()

    total = sum_b[z_here].astype(WIDE)
    for i in range(1, layers):
        z = (z_here + i) % layers
        from_layer(z).wait_recv()
        total = total + got_c[z].astype(WIDE)
    done_ref[...] = total

    own(0).wait()
    own(1).wait()
    for i in range(1, spots):
        to_spot((spot + i) % spots).wait_send()
    for i in range(1, layers):
        to_layer((z_here + i) % layers).wait_send()

    @pl.loop(1, n)
    def _(r):
        p = (me + r) % n
        for which in range(2):
            grads_to(which, p).wait_send()
            grads_from(which, p).wait_recv()


def finish_kernel(
    experts, done_ref, gin_ref, gback_ref, tok_ref, res_ref,
    din_ref, dback_ref, dtok_ref, result_ref, dqkv_ref, dwout_ref, drouter_ref, dbback_ref,
    dbin_ref, *vec_refs,
):
    din_ref[...] = gin_ref[...].astype(WIDE)
    dback_ref[...] = gback_ref[...].astype(WIDE)
    dtok_ref[...] = tok_ref[...]
    result_ref[...] = res_ref[...]

    @pl.when(pl.program_id(0) == 0)
    def _():
        dense_blk, width = dwout_ref.shape
        for j in range(3):
            dqkv_ref[j] = done_ref[:, j * width : (j + 1) * width]
        dwout_ref[...] = done_ref[:, 3 * width : 4 * width]
        misc = done_ref[:, 4 * width : 4 * width + 128]
        drouter_ref[...] = misc[:, :experts]
        dbback_ref[...] = misc[:, experts : 2 * experts]
        diagonal = iota((dense_blk, dense_blk), 0) == iota((dense_blk, dense_blk), 1)
        for i, vec in enumerate(vec_refs):
            column = misc[:, 2 * experts + i : 2 * experts + i + 1]
            vec[...] = jnp.sum(jnp.where(diagonal, column, 0.0), axis=0, keepdims=True)
        lines = dbin_ref.shape[1] // 128
        for i in range(dense_blk):
            dbin_ref[i // lines : i // lines + 1, (i % lines) * 128 : (i % lines + 1) * 128] = (
                done_ref[i : i + 1, 4 * width + 128 : 4 * width + 256]
            )


VMEM = pl.BlockSpec(memory_space=pltpu.VMEM)


def make_owner_device(dp, tn):
    n = dp * tn

    def per_device(
        tokens, cotangent, ln1_scale, ln1_shift, w_qkv, w_out, out_bias, ln2_scale, ln2_shift,
        w_router, w_in, b_in, w_back, b_back, choices, slots,
    ):
        rows, width = tokens.shape
        images = rows // SEQ
        experts, blk_d, blk_f = w_in.shape
        ff = blk_f * tn
        dense_blk = w_out.shape[0]
        places = experts * MAIN
        landed = n // 4 * GROUP
        shape = jax.ShapeDtypeStruct

        cols = 4 * width + 256
        per_layer = dp // 4

        hbm = pl.BlockSpec(memory_space=pl.ANY)
        saved = [
            ((per_layer, 2, 2, tn, dense_blk, cols), LOW),
            ((rows, 3 * width), LOW),
            ((rows, width), LOW),
            ((rows, 128), WIDE),
            ((rows, width), WIDE),
            ((rows, width), LOW),
            ((rows, 128), WIDE),
            ((rows, 128), jnp.int32),
        ]
        weight_shape = (n, blk_d, blk_f)
        out_home, back_home, tails_home, dense, qkv, att, lse, mid, two, route, col, d_first, d_second, d_b = pl.pallas_call(
            functools.partial(layer_kernel, dp, images, experts),
            out_shape=(
                shape((places, width), LOW),
                shape((places, width), LOW),
                shape((n, 8, 128), LOW),
                *[shape(*s) for s in saved],
                shape(weight_shape, LOW),
                shape(weight_shape, LOW),
                shape((1, ff), WIDE),
            ),
            in_specs=[VMEM] * 14 + [hbm, hbm],
            out_specs=(hbm,) * 13 + (VMEM,),
            scratch_shapes=[
                *[pltpu.VMEM(*saved[i]) for i in (0, 3, 4, 6, 7)],
                pltpu.VMEM((dense_blk, cols), LOW),
                pltpu.VMEM((2, rows), jnp.int32),
                pltpu.VMEM((2, 4, blk_d, blk_f), WIDE),
                pltpu.VMEM(weight_shape, LOW),
                pltpu.VMEM(weight_shape, LOW),
                pltpu.VMEM((tn, width, blk_f), LOW),
                pltpu.VMEM((tn, width, blk_f), LOW),
                pltpu.VMEM((1, ff), WIDE),
                pltpu.VMEM((places, width), LOW),
                pltpu.VMEM((places, width), LOW),
                pltpu.VMEM((landed, width), LOW),
                pltpu.VMEM((landed, width), LOW),
                pltpu.VMEM((landed, ff), LOW),
                pltpu.VMEM((landed, ff), LOW),
                pltpu.VMEM((places, width), LOW),
                pltpu.VMEM((n, rows), LOW),
                pltpu.VMEM((2, rows), jnp.int32),
                *[pltpu.VMEM((n, 8, 128), LOW)] * 5,
                pltpu.SemaphoreType.DMA((2,)),
                pltpu.SemaphoreType.DMA((2, n)),
                pltpu.SemaphoreType.DMA((2, n)),
                pltpu.SemaphoreType.DMA((n,)),
                pltpu.SemaphoreType.DMA((n,)),
                pltpu.SemaphoreType.DMA((n,)),
                pltpu.SemaphoreType.DMA((n,)),
                pltpu.SemaphoreType.DMA((2, n)),
                pltpu.SemaphoreType.DMA((2, n)),
                pltpu.SemaphoreType.DMA((3, n)),
                pltpu.SemaphoreType.DMA((3, n)),
                pltpu.SemaphoreType.DMA((per_layer,)),
                pltpu.SemaphoreType.DMA((per_layer,)),
                pltpu.SemaphoreType.DMA((2 * tn,)),
                pltpu.SemaphoreType.DMA((2 * tn,)),
                pltpu.SemaphoreType.DMA((2,)),
                pltpu.SemaphoreType.DMA((10,)),
                pltpu.SemaphoreType.DMA((10,)),
            ],
            compiler_params=pltpu.CompilerParams(
                vmem_limit_bytes=63 * 2**20, collective_id=1, has_side_effects=True
            ),
            cost_estimate=pl.CostEstimate(
                flops=12 * places * width * ff, bytes_accessed=10 * places * width, transcendentals=0
            ),
            name="layer",
        )(
            tokens, cotangent, choices.T, slots.T,
            *[v.reshape(1, dense_blk) for v in (ln1_scale, ln1_shift, out_bias, ln2_scale, ln2_shift)],
            w_qkv, w_out, w_router, b_back.T, b_in, w_in, jnp.swapaxes(w_back, 1, 2),
        )
        dense = dense.reshape(width, cols)
        brought = (
            tokens, cotangent, dense, qkv, att, lse, mid, two, route, col, out_home, back_home,
            tails_home,
        )
        result, d_tok, done, grad_in, grad_back = pl.pallas_call(
            functools.partial(backward_kernel, dp, images, experts),
            out_shape=(
                shape((rows, width), LOW),
                shape((rows, width), WIDE),
                shape((dense_blk, cols), WIDE),
                shape((n, blk_d, blk_f), LOW),
                shape((n, blk_d, blk_f), LOW),
            ),
            in_specs=[hbm] * 13 + [VMEM] + [hbm] * 2,
            out_specs=(VMEM, VMEM, VMEM, hbm, hbm),
            scratch_shapes=[
                *[pltpu.VMEM(v.shape, v.dtype) for v in brought[:10]],
                pltpu.VMEM((places + 128, width), LOW),
                pltpu.VMEM((places + 128, width), LOW),
                pltpu.VMEM((n, 8, 128), LOW),
                pltpu.SemaphoreType.DMA((13,)),
                pltpu.VMEM((rows, width), LOW),
                pltpu.VMEM((rows, width), LOW),
                pltpu.VMEM((rows, 3 * width), LOW),
                pltpu.VMEM((dp // 2, 2, tn * dense_blk, cols), LOW),
                pltpu.VMEM((dp // 2, tn * dense_blk, cols), LOW),
                pltpu.VMEM((per_layer, 2 * tn, dense_blk, cols), LOW),
                pltpu.VMEM((2 * tn, per_layer, dense_blk, cols), LOW),
                pltpu.VMEM((per_layer, dense_blk, cols), LOW),
                pltpu.VMEM((per_layer, dense_blk, cols), LOW),
                pltpu.SemaphoreType.DMA((2, n)),
                pltpu.SemaphoreType.DMA((2, n)),
                pltpu.SemaphoreType.DMA((2,)),
                pltpu.SemaphoreType.DMA((2,)),
                pltpu.SemaphoreType.DMA((2 * tn,)),
                pltpu.SemaphoreType.DMA((2 * tn,)),
                pltpu.SemaphoreType.DMA((per_layer,)),
                pltpu.SemaphoreType.DMA((per_layer,)),
            ],
            compiler_params=pltpu.CompilerParams(
                vmem_limit_bytes=60 * 2**20, collective_id=2, has_side_effects=True
            ),
            cost_estimate=pl.CostEstimate(
                flops=6 * places * rows * width + 20 * rows * width * width,
                bytes_accessed=40 * rows * width, transcendentals=0,
            ),
            name="backward",
        )(
            *brought, d_b, d_first, d_second,
        )
        steps = 8
        tok_rows = rows // 7

        def whole(dims):
            return pl.BlockSpec(dims, lambda i: (0,) * len(dims))

        piece = pl.BlockSpec((n // steps, blk_d, blk_f), lambda i: (i, 0, 0))
        tok_piece = pl.BlockSpec((tok_rows, width), lambda i: (jnp.minimum(i, 6), 0))
        vec = (1, dense_blk)
        small = [w_qkv.shape, w_out.shape, w_router.shape, (dense_blk, experts), b_in.shape] + [vec] * 5
        grad_in, grad_back, d_tok, result, *rest = pl.pallas_call(
            functools.partial(finish_kernel, experts),
            grid=(steps,),
            out_shape=(
                shape(weight_shape, WIDE),
                shape(weight_shape, WIDE),
                shape((rows, width), WIDE),
                shape((rows, width), LOW),
                *[shape(d, WIDE) for d in small],
            ),
            in_specs=[whole(done.shape), piece, piece, tok_piece, tok_piece],
            out_specs=(piece, piece, tok_piece, tok_piece, *[whole(d) for d in small]),
            name="finish",
        )(done, grad_in, grad_back, d_tok, result)
        d_qkv, d_wout, d_router, d_bback, d_bin, *vecs = rest
        d_vecs = [v.reshape(dense_blk) for v in vecs]
        return (
            result,
            d_tok,
            d_vecs[0],
            d_vecs[1],
            d_qkv,
            d_wout,
            d_vecs[2],
            d_vecs[3],
            d_vecs[4],
            d_router,
            grad_in,
            d_bin,
            jnp.swapaxes(grad_back, 1, 2),
            d_bback.T,
        )

    return per_device


def make_per_device(dp, tn):
    everyone = ("dp", "tensor")
    n = dp * tn

    def per_device(
        tokens,
        cotangent,
        ln1_scale,
        ln1_shift,
        w_qkv,
        w_out,
        out_bias,
        ln2_scale,
        ln2_shift,
        w_router,
        w_in,
        b_in,
        w_back,
        b_back,
        choices,
        slots,
    ):
        rows_here, width = tokens.shape
        images = rows_here // SEQ
        experts, blk_d, blk_f = w_in.shape
        ff = blk_f * tn
        dense_blk = w_out.shape[0]
        whole = experts % n == 0
        owners = n if whole else dp
        owned = experts // owners
        expert_axes = ("tensor", "dp") if whole else ("dp",)
        slot_total = experts * CAP
        score_scale = HD ** (-0.5)

        w_pack = jnp.stack([w_in.astype(LOW), jnp.swapaxes(w_back, 1, 2).astype(LOW)], axis=1)
        w_all = lax.all_to_all(w_pack, expert_axes, split_axis=0, concat_axis=0, tiled=True)
        f_parts = tn if whole else 1
        w_all = w_all.reshape(f_parts, dp, owned, 2, blk_d, blk_f)
        w_all = w_all.transpose(3, 2, 1, 4, 0, 5).reshape(2, owned, width, f_parts * blk_f)
        first_w, second_wt = w_all[0], w_all[1]

        vec_rows = jnp.stack([ln1_scale, ln1_shift, out_bias, ln2_scale, ln2_shift])
        pieces = [
            w_qkv.reshape(-1),
            w_out.reshape(-1),
            w_router.reshape(-1),
            b_back.reshape(-1),
            b_in.reshape(-1),
            vec_rows.reshape(-1),
        ]
        sizes = [p.shape[0] for p in pieces]
        total = sum(sizes)
        pad = -total % 512
        packed = jnp.concatenate([p.astype(LOW) for p in pieces] + [jnp.zeros((pad,), LOW)])
        gathered = lax.all_gather(packed.reshape(-1, 512), everyone, axis=0, tiled=False)
        gathered = gathered.reshape(n, -1)
        offs = [sum(sizes[:i]) for i in range(len(sizes))]
        part = [gathered[:, o : o + s] for o, s in zip(offs, sizes)]
        qkv_w = part[0].reshape(n, 3, dense_blk, width).swapaxes(0, 1).reshape(3, width, width)
        out_w = part[1].reshape(width, width)
        router = part[2].reshape(width, experts)
        bias_back = part[3].reshape(n, experts, -1).swapaxes(0, 1).reshape(experts, width)
        bias_back = bias_back.astype(WIDE)
        in_b = part[4].reshape(dp, tn, experts // dp, blk_f).swapaxes(1, 2).reshape(experts, ff)
        vecs = part[5].reshape(n, 5, -1).swapaxes(0, 1).reshape(5, width).astype(WIDE)
        gain_one, shift_one, bias_attn, gain_two, shift_two = vecs
        if whole:
            mine = lax.axis_index("tensor") * dp + lax.axis_index("dp")
            my_b = lax.dynamic_slice(in_b, (mine * owned, 0), (owned, ff)).astype(WIDE)
        else:
            my_b = lax.dynamic_slice(
                in_b,
                (lax.axis_index("dp") * owned, lax.axis_index("tensor") * blk_f),
                (owned, blk_f),
            ).astype(WIDE)

        residual = tokens.astype(WIDE)
        normed_one = norm_affine(residual, gain_one, shift_one).astype(LOW)
        projected = jnp.einsum(
            "td,jde->jte", normed_one, qkv_w, preferred_element_type=WIDE
        ).astype(LOW)
        head_query = projected[0].reshape(images, SEQ, H, HD)
        head_key = projected[1].reshape(images, SEQ, H, HD)
        head_value = projected[2].reshape(images, SEQ, H, HD)
        raw_scores = jnp.einsum(
            "ishd,ithd->ihst", head_query, head_key, preferred_element_type=WIDE
        )
        scaled = raw_scores * score_scale
        row_top = jnp.max(scaled, axis=-1, keepdims=True)
        log_total = row_top + jnp.log(jnp.sum(jnp.exp(scaled - row_top), axis=-1, keepdims=True))
        weights_att = jnp.exp(scaled - log_total).astype(LOW)
        attended = (
            jnp.einsum("ihst,ithd->ishd", weights_att, head_value, preferred_element_type=WIDE)
            .astype(LOW)
            .reshape(rows_here, width)
        )
        attn_sum = jnp.dot(attended, out_w, preferred_element_type=WIDE)
        middle = residual + attn_sum + bias_attn
        normed_two = norm_affine(middle, gain_two, shift_two).astype(LOW)
        route_p = jax.nn.softmax(jnp.dot(normed_two, router, preferred_element_type=WIDE), axis=-1)

        expert_ids = jnp.arange(experts, dtype=jnp.int32)
        chosen = [
            (choices[:, k : k + 1] == expert_ids[None, :]).astype(WIDE) for k in range(2)
        ]
        gate_vals = jnp.concatenate(
            [jnp.sum(route_p * c, axis=1, keepdims=True) for c in chosen], axis=1
        )
        kept_pair = (slots >= 0).astype(WIDE)
        target = jnp.where(slots >= 0, choices * CAP + slots, -1)
        places = jnp.arange(slot_total, dtype=jnp.int32)
        by_slot = [target[:, k][None, :] == places[:, None] for k in range(2)]
        spread_mat = (by_slot[0] | by_slot[1]).astype(LOW)
        by_token = [target[:, k : k + 1] == places[None, :] for k in range(2)]
        pair_weight = gate_vals * kept_pair
        slot_gate = jnp.sum(
            jnp.where(by_slot[0], pair_weight[:, 0][None, :], 0.0)
            + jnp.where(by_slot[1], pair_weight[:, 1][None, :], 0.0),
            axis=1,
            keepdims=True,
        )
        both = jnp.dot(
            spread_mat,
            jnp.concatenate([normed_two, cotangent], axis=1),
            preferred_element_type=WIDE,
        )
        buffer = both[:, :width].astype(LOW).reshape(experts, CAP, width)
        slot_grad = slot_gate * both[:, width:]
        grad_bias_back = jnp.sum(slot_grad.reshape(experts, CAP, width), axis=1)
        slot_grad_low = slot_grad.astype(LOW).reshape(experts, CAP, width)

        def out_to_experts(rows):
            width_c = rows.shape[1]
            if not whole:
                rows = lax.all_gather(rows, "tensor", axis=1, tiled=True)
            rows = lax.all_to_all(rows, expert_axes, split_axis=0, concat_axis=0, tiled=True)
            return rows.reshape(owners, owned, -1, width)

        def back_to_tokens(rows):
            rows = rows.reshape(experts, -1, width)
            rows = lax.all_to_all(rows, expert_axes, split_axis=0, concat_axis=0, tiled=True)
            if not whole:
                rows = lax.psum_scatter(rows, "tensor", scatter_dimension=1, tiled=True)
            return rows

        sent = out_to_experts(jnp.concatenate([buffer, slot_grad_low], axis=1))
        group = sent.shape[2] // (2 * CAP)
        sent = sent.reshape(owners, owned, group, 2, CAP, width).transpose(3, 1, 0, 2, 4, 5)
        sent = sent.reshape(2, owned, owners * group * CAP, width)
        all_slots, slot_grad_all = sent[0], sent[1]

        pre_act = (
            jnp.einsum("ecd,edf->ecf", all_slots, first_w, preferred_element_type=WIDE)
            + my_b[:, None, :]
        )
        hidden, gelu_pull = jax.vjp(lambda member: jax.nn.gelu(member, approximate=True), pre_act)
        hidden = hidden.astype(LOW)
        expert_sum = jnp.einsum("ecf,edf->ecd", hidden, second_wt, preferred_element_type=WIDE)
        grad_hidden = jnp.einsum("ecd,edf->ecf", slot_grad_all, second_wt, preferred_element_type=WIDE)
        grad_pre = gelu_pull(grad_hidden)[0].astype(LOW)
        grad_slots_all = jnp.einsum("ecf,edf->ecd", grad_pre, first_w, preferred_element_type=WIDE)
        returned = jnp.stack([expert_sum.astype(LOW), grad_slots_all.astype(LOW)])
        returned = returned.reshape(2, owned, owners, group, CAP, width).transpose(2, 1, 3, 0, 4, 5)
        returned = returned.reshape(owners * owned, group * 2 * CAP, width)
        home = back_to_tokens(returned).reshape(experts, 2, CAP, width)
        expert_home = home[:, 0].reshape(slot_total, width)
        grad_home = home[:, 1].reshape(slot_total, width)

        grad_first_b = jnp.sum(grad_pre.astype(WIDE), axis=1)
        grad_first_w = jnp.einsum("ecd,ecf->edf", all_slots, grad_pre, preferred_element_type=WIDE)
        grad_second_t = jnp.einsum("ecd,ecf->edf", slot_grad_all, hidden, preferred_element_type=WIDE)
        g_pack = jnp.stack([grad_first_w.astype(LOW), grad_second_t.astype(LOW)])
        g_pack = g_pack.reshape(2, owned, dp, blk_d, f_parts, blk_f).transpose(4, 2, 1, 0, 3, 5)
        g_pack = g_pack.reshape(f_parts * dp * owned, 2, blk_d, blk_f)
        g_home = lax.all_to_all(g_pack, expert_axes, split_axis=0, concat_axis=0, tiled=True)
        g_home = g_home.reshape(experts, 2, blk_d, blk_f).astype(WIDE)
        grad_w_in = g_home[:, 0]
        grad_w_back = jnp.swapaxes(g_home[:, 1], 1, 2)

        picked = []
        for k in range(2):
            rows = jnp.dot(by_token[k].astype(LOW), expert_home, preferred_element_type=WIDE)
            bias_rows = jnp.dot(
                chosen[k].astype(LOW), bias_back.astype(LOW), preferred_element_type=WIDE
            )
            picked.append((rows + bias_rows) * kept_pair[:, k : k + 1])
        result = (
            middle + gate_vals[:, 0:1] * picked[0] + gate_vals[:, 1:2] * picked[1]
        ).astype(LOW)
        grad_out = cotangent.astype(WIDE)
        grad_probs = sum(
            jnp.sum(grad_out * picked[k], axis=1, keepdims=True) * chosen[k] for k in range(2)
        )
        gather_mat = (by_token[0] | by_token[1]).astype(LOW)
        grad_normed_two = jnp.dot(gather_mat, grad_home, preferred_element_type=WIDE)
        grad_logits = route_p * (grad_probs - jnp.sum(grad_probs * route_p, axis=-1, keepdims=True))
        grad_normed_two = grad_normed_two + jnp.dot(
            grad_logits, router.astype(WIDE).T, precision=lax.Precision.HIGHEST
        )
        grad_router = jnp.dot(
            normed_two.astype(WIDE).T, grad_logits, precision=lax.Precision.HIGHEST
        )
        _, pull_two = jax.vjp(norm_affine, middle, gain_two, shift_two)
        grad_mid_norm, grad_gain_two, grad_shift_two = pull_two(grad_normed_two)
        grad_middle = grad_out + grad_mid_norm
        grad_bias_attn = jnp.sum(grad_middle, axis=0)
        grad_mid_low = grad_middle.astype(LOW)
        grad_att = jnp.einsum(
            "td,ed->te", grad_mid_low, out_w, preferred_element_type=WIDE
        ).astype(LOW)
        grad_out_w = jnp.einsum("te,td->ed", attended, grad_mid_low, preferred_element_type=WIDE)
        grad_att_heads = grad_att.reshape(images, SEQ, H, HD)
        probs_again = jnp.exp(
            jnp.einsum("ishd,ithd->ihst", head_query, head_key, preferred_element_type=WIDE)
            * score_scale
            - log_total
        )
        grad_weights = jnp.einsum(
            "ishd,ithd->ihst", grad_att_heads, head_value, preferred_element_type=WIDE
        )
        row_delta = jnp.sum(grad_weights * probs_again, axis=-1, keepdims=True)
        grad_raw = (probs_again * (grad_weights - row_delta) * score_scale).astype(LOW)
        grad_value = jnp.einsum(
            "ihst,ishd->ithd",
            probs_again.astype(LOW),
            grad_att_heads,
            preferred_element_type=WIDE,
        )
        grad_query = jnp.einsum("ihst,ithd->ishd", grad_raw, head_key, preferred_element_type=WIDE)
        grad_key = jnp.einsum("ihst,ishd->ithd", grad_raw, head_query, preferred_element_type=WIDE)
        grad_proj = jnp.stack(
            [
                grad_query.astype(LOW).reshape(rows_here, width),
                grad_key.astype(LOW).reshape(rows_here, width),
                grad_value.astype(LOW).reshape(rows_here, width),
            ]
        )
        grad_qkv_w = jnp.einsum("td,jte->jde", normed_one, grad_proj, preferred_element_type=WIDE)
        grad_normed_one = jnp.einsum("jte,jde->td", grad_proj, qkv_w, preferred_element_type=WIDE)
        _, pull_one = jax.vjp(norm_affine, residual, gain_one, shift_one)
        grad_resid_norm, grad_gain_one, grad_shift_one = pull_one(grad_normed_one)
        grad_tokens = grad_middle + grad_resid_norm

        if whole:
            row_b = jnp.zeros((experts, ff), WIDE)
            row_b = lax.dynamic_update_slice(row_b, grad_first_b, (mine * owned, 0))
        else:
            row_b = jnp.zeros((experts, ff), WIDE)
            row_b = lax.dynamic_update_slice(
                row_b,
                grad_first_b,
                (lax.axis_index("dp") * owned, lax.axis_index("tensor") * blk_f),
            )
        vec_grads = jnp.stack(
            [grad_gain_one, grad_shift_one, grad_bias_attn, grad_gain_two, grad_shift_two]
        )
        out_pieces = [
            grad_qkv_w.reshape(3, n, dense_blk, width).swapaxes(0, 1).reshape(n, -1),
            grad_out_w.reshape(n, -1),
            grad_router.reshape(n, -1),
            grad_bias_back.reshape(experts, n, -1).swapaxes(0, 1).reshape(n, -1),
            row_b.reshape(dp, experts // dp, tn, blk_f).swapaxes(1, 2).reshape(n, -1),
            vec_grads.reshape(5, n, -1).swapaxes(0, 1).reshape(n, -1),
        ]
        out_pack = jnp.concatenate(
            [p.astype(LOW) for p in out_pieces] + [jnp.zeros((n, pad), LOW)], axis=1
        )
        out_all = lax.all_to_all(
            out_pack.reshape(n, -1, 512), everyone, split_axis=0, concat_axis=0, tiled=True
        )
        summed = jnp.sum(out_all.astype(WIDE), axis=0).reshape(-1)
        done = [summed[o : o + s] for o, s in zip(offs, sizes)]
        vec_done = done[5].reshape(5, -1)
        return (
            result,
            grad_tokens,
            vec_done[0],
            vec_done[1],
            done[0].reshape(w_qkv.shape),
            done[1].reshape(w_out.shape),
            vec_done[2],
            vec_done[3],
            vec_done[4],
            done[2].reshape(w_router.shape),
            grad_w_in,
            done[4].reshape(b_in.shape),
            grad_w_back,
            done[3].reshape(b_back.shape),
        )

    return per_device


def solution(mesh):
    everyone = ("dp", "tensor")
    in_specs = (
        P(everyone, None),
        P(everyone, None),
        P(everyone),
        P(everyone),
        P(None, everyone, None),
        P(everyone, None),
        P(everyone),
        P(everyone),
        P(everyone),
        P(everyone, None),
        P(None, "dp", "tensor"),
        P("dp", "tensor"),
        P(None, "tensor", "dp"),
        P(None, everyone),
        P(everyone, None),
        P(everyone, None),
    )
    out_specs = in_specs[:2] + in_specs[2:14]
    dp, tn = mesh.shape["dp"], mesh.shape["tensor"]

    def chosen(*args):
        one_each = args[10].shape[0] == dp * tn and dp % 4 == 0
        return (make_owner_device if one_each else make_per_device)(dp, tn)(*args)

    return jax.shard_map(
        chosen,
        mesh=mesh,
        in_specs=in_specs,
        out_specs=out_specs,
        check_vma=False,
    )
```

profile of v0, /device:TPU:13, one launch (start us, length us, event | category | flops | bytes accessed | tf_op | source)
XLA Modules:
  0.0 426.1 jit_solution(5826411703016204457)
XLA Ops:
  0.7 306.7 %layer.1 = (bf16[2048,512]{1,0:T(8,128)(2,1)}, bf16[2048,512]{1,0:T(8,128)(2,1)}, bf16[32,8,128]{2,1,0:T(8,128)(2,1)}, bf16[4,2,2,2,16,2304]{5,4,3,2,1,0:T(8,128...) custom-call(bf16[784,512]{1,0:T(8,128)(2,1)} %tok_in.1, ...), custom_call_target="tpu_custom_call" | custom-call | flops 25769803776 | bytes 10485760 | tf_op jit(solution)/shard_map/layer/pallas_call | solution.py:922
  307.4 109.4 %backward.1 = (bf16[784,512]{1,0:T(8,128)(2,1)}, f32[784,512]{1,0:T(8,128)}, f32[16,2304]{1,0:T(8,128)}, bf16[32,32,1024]{2,1,0:T(8,128)(2,1)}, bf16[32,32,1024]{2,1,0:T(8,128)(2,1)}) custom-call(bf16[784,512]{1,0:T(8,128)(2,1)} %tok_in.1, bf16[784,512]{1,0:T(8,128)(2,1)} %cot_in.1, bf16[512,2304]{1,0:T(8,128)(2,1)} %bitcast.33, ...), custom_call_target="tpu_custom_call" | custom-call | flops 9042919424 | bytes 16056320 | tf_op jit(solution)/shard_map/backward/pallas_call | solution.py:991
  416.8 9.1 %finish.1 = (f32[32,32,1024]{2,1,0:T(8,128)}, f32[32,32,1024]{2,1,0:T(8,128)}, f32[784,512]{1,0:T(8,128)}, bf16[784,512]{1,0:T(8,128)(2,1)}, f32[3,16,512]{2,1,0...) custom-call(f32[16,2304]{1,0:T(8,128)} %get-tuple-element.61.done_re, ...), custom_call_target="tpu_custom_call" | custom-call | tf_op jit(solution)/shard_map/finish/pallas_call | solution.py:1047
where the time goes:
time: 427 us; the launch traced here: 426 us
  Pallas kernels  425 us (100%)
    pallas_call x1, Pallas kernels, per_device(): pl.pallas_call(functools.partial(layer_kernel, dp, images, experts), out_...  307 us
    pallas_call x1, Pallas kernels, per_device(): pl.pallas_call(functools.partial(backward_kernel, dp, images, experts), o...  109 us
    pallas_call x1, Pallas kernels, per_device(): pl.pallas_call(functools.partial(finish_kernel, experts), grid=(steps,),...  9.11 us

commit v1 on v0

--- a/solution.py
+++ b/solution.py
@@ -176,12 +176,26 @@
         place = block(me) if which in (1, 2) else landing(me)
         return pltpu.make_async_copy(src.at[block(me)], dst.at[place], own_sem.at[which])
 
-    def to_layer(z, source):
+    near, across = z_here + 1 - 2 * (z_here % 2), (z_here + 2) % layers
+
+    def shard_at(source):
+        return dense_ref.at[source, y_here, core, t_here]
+
+    def to_layer(src, z, source, place):
         return pltpu.make_async_remote_copy(
-            src_ref=shard_ref, dst_ref=dense_ref.at[source, y_here, core, t_here],
-            send_sem=c_send.at[z], recv_sem=c_recv.at[source],
+            src_ref=src, dst_ref=shard_at(source),
+            send_sem=c_send.at[place], recv_sem=c_recv.at[source],
             device_id=((z * 2 + y_here) * 2 + core, t_here), device_id_type=MESH,
         )
+
+    def from_layer(source):
+        return to_layer(shard_at(source), near, source, 0)
+
+    layer_sends = (
+        to_layer(shard_ref, near, z_here, 0),
+        to_layer(shard_ref, across, z_here, 1),
+        to_layer(shard_at(across), near, across, 2),
+    )
 
     def to_spot(s, source):
         return pltpu.make_async_remote_copy(
@@ -252,8 +266,8 @@
     own_shard.start()
     db_ref[...] = jnp.zeros_like(db_ref)
     pl.semaphore_wait(barrier, n - 1)
-    for i in range(1, layers):
-        to_layer((z_here + i) % layers, z_here).start()
+    layer_sends[1].start()
+    layer_sends[0].start()
 
     def send_weights(which):
         low = (low_first, low_second)[which]
@@ -277,13 +291,14 @@
         own_weights(which).start()
 
     send_weights(0)
+    from_layer(across).wait_recv()
+    layer_sends[2].start()
+    send_weights(1)
     own_shard.wait()
-    for i in range(1, layers):
-        z = (z_here + i) % layers
-        to_layer(z, z).wait_recv()
+    from_layer(near).wait_recv()
+    from_layer((near + 2) % layers).wait_recv()
     for i in range(1, spots):
         to_spot((spot + i) % spots, spot).start()
-    send_weights(1)
 
     some = 8
     big = some * MAIN
@@ -551,8 +566,8 @@
     to_core(core).wait_send()
     for i in range(1, spots):
         to_spot((spot + i) % spots, spot).wait_send()
-    for i in range(1, layers):
-        to_layer((z_here + i) % layers, z_here).wait_send()
+    for copy in layer_sends:
+        copy.wait_send()
 
     @pl.loop(1, n)
     def _(r):
@@ -621,19 +636,20 @@
             device_id=((z_here * 2 + s // tn) * 2 + core, s % tn), device_id_type=MESH,
         )
 
-    def to_layer(z):
+    near, across = z_here + 1 - 2 * (z_here % 2), (z_here + 2) % layers
+
+    def to_layer(src, z, place):
         return pltpu.make_async_remote_copy(
-            src_ref=sum_b.at[z], dst_ref=got_c.at[z_here],
-            send_sem=c_send.at[z], recv_sem=c_recv.at[z_here],
+            src_ref=src, dst_ref=got_c.at[place],
+            send_sem=c_send.at[place], recv_sem=c_recv.at[place],
             device_id=((z * 2 + y_here) * 2 + core, t_here), device_id_type=MESH,
         )
 
-    def from_layer(z):
-        return pltpu.make_async_remote_copy(
-            src_ref=sum_b.at[z], dst_ref=got_c.at[z],
-            send_sem=c_send.at[z], recv_sem=c_recv.at[z],
-            device_id=((z * 2 + y_here) * 2 + core, t_here), device_id_type=MESH,
-        )
+    layer_sends = (
+        to_layer(sum_b.at[(near + 2) % layers], near, 0),
+        to_layer(sum_b.at[near], near, 1),
+        to_layer(got_c.at[3], across, 2),
+    )
 
     slots_main = out_in.shape[0]
     moves = (
@@ -826,26 +842,33 @@
         from_spot(s).wait_recv()
         total = total + got_b[s].astype(WIDE)
     sum_b[...] = total.astype(LOW)
-    for i in range(1, layers):
-        to_layer((z_here + i) % layers).start()
-
-    @pl.loop(3 * n // 4, n)
+    layer_sends[0].start()
+    layer_sends[1].start()
+
+    @pl.loop(3 * n // 4, 7 * n // 8)
     def _(r):
         grads_to(1, (me + r) % n).start()
 
-    total = sum_b[z_here].astype(WIDE)
-    for i in range(1, layers):
-        z = (z_here + i) % layers
-        from_layer(z).wait_recv()
-        total = total + got_c[z].astype(WIDE)
+    layer_sends[0].wait_recv()
+    got_c[3] = (sum_b[across].astype(WIDE) + got_c[0].astype(WIDE)).astype(LOW)
+    layer_sends[2].start()
+
+    @pl.loop(7 * n // 8, n)
+    def _(r):
+        grads_to(1, (me + r) % n).start()
+
+    layer_sends[1].wait_recv()
+    total = sum_b[z_here].astype(WIDE) + got_c[1].astype(WIDE)
+    layer_sends[2].wait_recv()
+    total = total + got_c[2].astype(WIDE)
     done_ref[...] = total
 
     own(0).wait()
     own(1).wait()
     for i in range(1, spots):
         to_spot((spot + i) % spots).wait_send()
-    for i in range(1, layers):
-        to_layer((z_here + i) % layers).wait_send()
+    for copy in layer_sends:
+        copy.wait_send()
 
     @pl.loop(1, n)
     def _(r):
@@ -858,31 +881,59 @@
 def finish_kernel(
     experts, done_ref, gin_ref, gback_ref, tok_ref, res_ref,
     din_ref, dback_ref, dtok_ref, result_ref, dqkv_ref, dwout_ref, drouter_ref, dbback_ref,
-    dbin_ref, *vec_refs,
+    dbin_ref, *refs,
 ):
-    din_ref[...] = gin_ref[...].astype(WIDE)
-    dback_ref[...] = gback_ref[...].astype(WIDE)
-    dtok_ref[...] = tok_ref[...]
-    result_ref[...] = res_ref[...]
-
-    @pl.when(pl.program_id(0) == 0)
-    def _():
-        dense_blk, width = dwout_ref.shape
-        for j in range(3):
-            dqkv_ref[j] = done_ref[:, j * width : (j + 1) * width]
-        dwout_ref[...] = done_ref[:, 3 * width : 4 * width]
-        misc = done_ref[:, 4 * width : 4 * width + 128]
-        drouter_ref[...] = misc[:, :experts]
-        dbback_ref[...] = misc[:, experts : 2 * experts]
-        diagonal = iota((dense_blk, dense_blk), 0) == iota((dense_blk, dense_blk), 1)
-        for i, vec in enumerate(vec_refs):
-            column = misc[:, 2 * experts + i : 2 * experts + i + 1]
-            vec[...] = jnp.sum(jnp.where(diagonal, column, 0.0), axis=0, keepdims=True)
-        lines = dbin_ref.shape[1] // 128
-        for i in range(dense_blk):
-            dbin_ref[i // lines : i // lines + 1, (i % lines) * 128 : (i % lines + 1) * 128] = (
-                done_ref[i : i + 1, 4 * width + 128 : 4 * width + 256]
-            )
+    vec_refs, (low_ref, wide_ref, tok_held, res_held, in_sem, out_sem) = refs[:5], refs[5:]
+    pieces = in_sem.shape[0] - 2
+    each = low_ref.shape[0] // pieces
+    n = gin_ref.shape[0]
+
+    def bring(i):
+        if i >= pieces:
+            src, dst = ((tok_ref, tok_held), (res_ref, res_held))[i - pieces]
+            return pltpu.make_async_copy(src, dst, in_sem.at[i])
+        src = (gin_ref, gback_ref)[i * each // n]
+        return pltpu.make_async_copy(
+            src.at[i * each % n : i * each % n + each],
+            low_ref.at[i * each : (i + 1) * each], in_sem.at[i],
+        )
+
+    def save(i):
+        if i >= pieces:
+            src, dst = ((tok_held, dtok_ref), (res_held, result_ref))[i - pieces]
+            return pltpu.make_async_copy(src, dst, out_sem.at[i])
+        dst = (din_ref, dback_ref)[i * each // n]
+        return pltpu.make_async_copy(
+            wide_ref.at[i * each : (i + 1) * each],
+            dst.at[i * each % n : i * each % n + each], out_sem.at[i],
+        )
+
+    for i in range(pieces + 2):
+        bring(i).start()
+    dense_blk, width = dwout_ref.shape
+    for j in range(3):
+        dqkv_ref[j] = done_ref[:, j * width : (j + 1) * width]
+    dwout_ref[...] = done_ref[:, 3 * width : 4 * width]
+    misc = done_ref[:, 4 * width : 4 * width + 128]
+    drouter_ref[...] = misc[:, :experts]
+    dbback_ref[...] = misc[:, experts : 2 * experts]
+    diagonal = iota((dense_blk, dense_blk), 0) == iota((dense_blk, dense_blk), 1)
+    for i, vec in enumerate(vec_refs):
+        column = misc[:, 2 * experts + i : 2 * experts + i + 1]
+        vec[...] = jnp.sum(jnp.where(diagonal, column, 0.0), axis=0, keepdims=True)
+    lines = dbin_ref.shape[1] // 128
+    for i in range(dense_blk):
+        dbin_ref[i // lines : i // lines + 1, (i % lines) * 128 : (i % lines + 1) * 128] = (
+            done_ref[i : i + 1, 4 * width + 128 : 4 * width + 256]
+        )
+    for i in range(pieces + 2):
+        bring(i).wait()
+        if i < pieces:
+            span = slice(i * each, (i + 1) * each)
+            wide_ref[span] = low_ref[span].astype(WIDE)
+        save(i).start()
+    for i in range(pieces + 2):
+        save(i).wait()
 
 
 VMEM = pl.BlockSpec(memory_space=pltpu.VMEM)
@@ -1034,19 +1085,10 @@
         )(
             *brought, d_b, d_first, d_second,
         )
-        steps = 8
-        tok_rows = rows // 7
-
-        def whole(dims):
-            return pl.BlockSpec(dims, lambda i: (0,) * len(dims))
-
-        piece = pl.BlockSpec((n // steps, blk_d, blk_f), lambda i: (i, 0, 0))
-        tok_piece = pl.BlockSpec((tok_rows, width), lambda i: (jnp.minimum(i, 6), 0))
         vec = (1, dense_blk)
         small = [w_qkv.shape, w_out.shape, w_router.shape, (dense_blk, experts), b_in.shape] + [vec] * 5
         grad_in, grad_back, d_tok, result, *rest = pl.pallas_call(
             functools.partial(finish_kernel, experts),
-            grid=(steps,),
             out_shape=(
                 shape(weight_shape, WIDE),
                 shape(weight_shape, WIDE),
@@ -1054,8 +1096,16 @@
                 shape((rows, width), LOW),
                 *[shape(d, WIDE) for d in small],
             ),
-            in_specs=[whole(done.shape), piece, piece, tok_piece, tok_piece],
-            out_specs=(piece, piece, tok_piece, tok_piece, *[whole(d) for d in small]),
+            in_specs=[VMEM] + [hbm] * 4,
+            out_specs=(hbm,) * 4 + (VMEM,) * len(small),
+            scratch_shapes=[
+                pltpu.VMEM((2 * n, blk_d, blk_f), LOW),
+                pltpu.VMEM((2 * n, blk_d, blk_f), WIDE),
+                pltpu.VMEM((rows, width), WIDE),
+                pltpu.VMEM((rows, width), LOW),
+                pltpu.SemaphoreType.DMA((18,)),
+                pltpu.SemaphoreType.DMA((18,)),
+            ],
             name="finish",
         )(done, grad_in, grad_back, d_tok, result)
         d_qkv, d_wout, d_router, d_bback, d_bin, *vecs = rest
@@ -1397,7 +1447,7 @@
     dp, tn = mesh.shape["dp"], mesh.shape["tensor"]
 
     def chosen(*args):
-        one_each = args[10].shape[0] == dp * tn and dp % 4 == 0
+        one_each = args[10].shape[0] == dp * tn and dp // 4 == 4 and dp % 4 == 0
         return (make_owner_device if one_each else make_per_device)(dp, tn)(*args)
 
     return jax.shard_map(

time: 427 us -> 422 us (0.988)
  no operation moved by 1% of the time
where the time goes in v1:
time: 422 us; the launch traced here: 421 us
  Pallas kernels  421 us (100%)
    pallas_call x1, Pallas kernels, per_device(): pl.pallas_call(functools.partial(layer_kernel, dp, images, experts), out_...  305 us
    pallas_call x1, Pallas kernels, per_device(): pl.pallas_call(functools.partial(backward_kernel, dp, images, experts), o...  107 us

profile of v1, /device:TPU:13, one launch (start us, length us, event | category | flops | bytes accessed | tf_op | source)
XLA Modules:
  0.0 421.5 jit_solution(7958463496014261382)
XLA Ops:
  0.7 305.4 %layer.1 = (bf16[2048,512]{1,0:T(8,128)(2,1)}, bf16[2048,512]{1,0:T(8,128)(2,1)}, bf16[32,8,128]{2,1,0:T(8,128)(2,1)}, bf16[4,2,2,2,16,2304]{5,4,3,2,1,0:T(8,128...) custom-call(bf16[784,512]{1,0:T(8,128)(2,1)} %tok_in.1, ...), custom_call_target="tpu_custom_call" | custom-call | flops 25769803776 | bytes 10485760 | tf_op jit(solution)/shard_map/layer/pallas_call | solution.py:973
  306.1 107.2 %backward.1 = (bf16[784,512]{1,0:T(8,128)(2,1)}, f32[784,512]{1,0:T(8,128)}, f32[16,2304]{1,0:T(8,128)}, bf16[32,32,1024]{2,1,0:T(8,128)(2,1)}, bf16[32,32,1024]{2,1,0:T(8,128)(2,1)}) custom-call(bf16[784,512]{1,0:T(8,128)(2,1)} %tok_in.1, bf16[784,512]{1,0:T(8,128)(2,1)} %cot_in.1, bf16[512,2304]{1,0:T(8,128)(2,1)} %bitcast.33, ...), custom_call_target="tpu_custom_call" | custom-call | flops 9042919424 | bytes 16056320 | tf_op jit(solution)/shard_map/backward/pallas_call | solution.py:1042
  413.3 8.0 %finish.1 = (f32[32,32,1024]{2,1,0:T(8,128)}, f32[32,32,1024]{2,1,0:T(8,128)}, f32[784,512]{1,0:T(8,128)}, bf16[784,512]{1,0:T(8,128)(2,1)}, f32[3,16,512]{2,1,0...) custom-call(f32[16,2304]{1,0:T(8,128)} %get-tuple-element.61.done_re, ...), custom_call_target="tpu_custom_call" | custom-call | tf_op jit(solution)/shard_map/finish/pallas_call | solution.py:1090

commit v2 on v1

--- a/solution.py
+++ b/solution.py
@@ -676,7 +676,7 @@
     def _(r):
         grads_to(0, (me + r) % n).start()
 
-    @pl.loop(1, 3 * n // 8)
+    @pl.loop(1, n // 2)
     def _(r):
         grads_to(1, (me + r) % n).start()
 
@@ -832,7 +832,7 @@
     for i in range(1, spots):
         to_spot((spot + i) % spots).start()
 
-    @pl.loop(3 * n // 8, 3 * n // 4)
+    @pl.loop(n // 2, 3 * n // 4)
     def _(r):
         grads_to(1, (me + r) % n).start()
 

time: 422 us -> 422 us (level)
  no operation moved by 1% of the time
where the time goes in v2:
time: 422 us; the launch traced here: 420 us
  Pallas kernels  420 us (100%)
    pallas_call x1, Pallas kernels, per_device(): pl.pallas_call(functools.partial(layer_kernel, dp, images, experts), out_...  305 us
    pallas_call x1, Pallas kernels, per_device(): pl.pallas_call(functools.partial(backward_kernel, dp, images, experts), o...  106 us

profile of v2, /device:TPU:13, one launch (start us, length us, event | category | flops | bytes accessed | tf_op | source)
XLA Modules:
  0.0 420.4 jit_solution(12270261329437220414)
XLA Ops:
  0.7 305.4 %layer.1 = (bf16[2048,512]{1,0:T(8,128)(2,1)}, bf16[2048,512]{1,0:T(8,128)(2,1)}, bf16[32,8,128]{2,1,0:T(8,128)(2,1)}, bf16[4,2,2,2,16,2304]{5,4,3,2,1,0:T(8,128...) custom-call(bf16[784,512]{1,0:T(8,128)(2,1)} %tok_in.1, ...), custom_call_target="tpu_custom_call" | custom-call | flops 25769803776 | bytes 10485760 | tf_op jit(solution)/shard_map/layer/pallas_call | solution.py:973
  306.1 106.1 %backward.1 = (bf16[784,512]{1,0:T(8,128)(2,1)}, f32[784,512]{1,0:T(8,128)}, f32[16,2304]{1,0:T(8,128)}, bf16[32,32,1024]{2,1,0:T(8,128)(2,1)}, bf16[32,32,1024]{2,1,0:T(8,128)(2,1)}) custom-call(bf16[784,512]{1,0:T(8,128)(2,1)} %tok_in.1, bf16[784,512]{1,0:T(8,128)(2,1)} %cot_in.1, bf16[512,2304]{1,0:T(8,128)(2,1)} %bitcast.33, ...), custom_call_target="tpu_custom_call" | custom-call | flops 9042919424 | bytes 16056320 | tf_op jit(solution)/shard_map/backward/pallas_call | solution.py:1042
  412.2 8.0 %finish.1 = (f32[32,32,1024]{2,1,0:T(8,128)}, f32[32,32,1024]{2,1,0:T(8,128)}, f32[784,512]{1,0:T(8,128)}, bf16[784,512]{1,0:T(8,128)(2,1)}, f32[3,16,512]{2,1,0...) custom-call(f32[16,2304]{1,0:T(8,128)} %get-tuple-element.61.done_re, ...), custom_call_target="tpu_custom_call" | custom-call | tf_op jit(solution)/shard_map/finish/pallas_call | solution.py:1090
